TPU v7x, 512 devices: a whole 4x8x8 slice. The times are simulated.
512 devices in a mesh: rows: 64 (over y, x, z_hi), cols: 8 (over z_lo, core).
Axes of the slice: x: 4, y: 8, z: 8 (z_hi: 2, z_lo: 4; z = z_hi * 4 + z_lo), core: 2. Of those that a mesh axis runs over, the one named last changes fastest.
Arguments:
- cross_kernel: float32 [65536, 1024], P('rows', 'cols'), may hold values from -6 to 6
- factor_panels: float32 [2, 512, 65536], P(None, 'cols', 'rows'), may hold values from -0.25 to 0.25
- block_inverses: float32 [2, 512, 512], P(None, 'cols'), may hold values from -0.5 to 1.5, as said below
Outputs:
- solved: float32 [65536, 1024], P('rows', 'cols')
Inputs may be any that keep to these rules, and one draw needn't show every extreme that they name: `block_inverses`: each block is lower triangular, with diagonal entries from 0.5 to 1.5.
All inputs are finite; a program needn't handle non-finite values.
Results may differ from a plain program's by a relative error of at most 0.000084.
Values sent between devices are 32-bit elements; how exact they have to be, the bound alone decides.
A program may use at most 64 MiB of HBM per device.

v0:
```python
import jax
import jax.numpy as jnp
from jax import lax
from jax.sharding import PartitionSpec as P

highest = lax.Precision.HIGHEST


def spread(array, axis, root):
    mine = lax.axis_index(axis) == root
    return lax.psum(jnp.where(mine, array, jnp.zeros_like(array)), axis)


def contract_rows(left, right):
    return lax.dot_general(
        left, right, (((0,), (0,)), ((), ())), precision=highest, preferred_element_type=jnp.float32
    )


def diagonal_solve(inverse_rows, rhs_block):
    return jnp.dot(
        lax.all_gather(inverse_rows, "cols", axis=0, tiled=True),
        rhs_block,
        precision=highest,
        preferred_element_type=jnp.float32,
    )


def share_block(solved_rows):
    return spread(solved_rows, "rows", 0)


def second_update(factor_rows, solved_rows):
    return contract_rows(lax.all_gather(factor_rows, "cols", axis=0, tiled=True), solved_rows)


def on_device(cross_kernel, factor_panels, block_inverses):
    width = block_inverses.shape[2]
    is_zero = lax.axis_index("rows") == 0
    first_factor = lax.all_gather(factor_panels[0], "cols", axis=0, tiled=True)
    first = share_block(diagonal_solve(block_inverses[0], cross_kernel[:width]))
    fresh = cross_kernel - contract_rows(first_factor, first)
    current = jnp.concatenate([jnp.where(is_zero, first, fresh[:width]), fresh[width:]], axis=0)
    second = share_block(diagonal_solve(block_inverses[1], current[width : 2 * width]))
    fresh = current - second_update(factor_panels[1], second)
    top = jnp.where(is_zero, current[:width], fresh[:width])
    middle = jnp.where(is_zero, second, fresh[width : 2 * width])
    return jnp.concatenate([top, middle, fresh[2 * width :]], axis=0)


def solution(mesh):
    in_specs = (P("rows", "cols"), P(None, "cols", "rows"), P(None, "cols", None))
    out_specs = P("rows", "cols")
    return jax.shard_map(
        on_device, mesh=mesh, in_specs=in_specs, out_specs=out_specs, check_vma=False
    )
```

profile of v0, /device:TPU:16, one launch (start us, length us, event | category | flops | bytes accessed | tf_op | source)
XLA Modules:
  0.0 1783.4 jit_solution(6935677184264947465)
XLA Ops:
  6.5 0.0 copy-start
  6.5 0.0 copy-start.3
  6.5 0.0 all-gather.9.cloned.1.call-start
  6.5 1.8 fusion.22
  8.3 0.0 all-gather.9.cloned.1.call-update
  8.3 0.0 all-reduce.3.cloned.1.call-start
  8.4 45.9 %all-gather.9.cloned.1.call-done = f32[1,512,512]{2,1,0:T(8,128)} async-done(((f32[1,64,512]{2,1,0:T(8,128)}), f32[1,512,512]{2,1,0:T(8,128)}) %all-gather.9.cloned.1.call-update) | async-done | bytes 1048592 | tf_op jit(solution)/shard_map/all_gather | solution.py:22
  54.3 3.0 convolution_select_fusion.1
  57.2 0.0 all-reduce.3.cloned.1.call-update
  57.3 0.0 all-gather.11.cloned.1.call-start
  57.3 0.0 copy-done.3
  57.3 0.8 fusion.21
  58.1 0.0 all-gather.11.cloned.1.call-update
  58.2 0.0 all-gather.13.cloned.1.call-start
  58.2 0.5 all-gather.13.cloned.1.call-update
  58.7 0.0 all-gather.15.cloned.1.call-start
  58.8 0.5 all-gather.15.cloned.1.call-update
  59.3 0.0 all-reduce.5.cloned.1.call-start
  59.4 790.3 %all-reduce.3.cloned.1.call-done = f32[512,128]{1,0:T(8,128)} async-done(((f32[512,128]{1,0:T(8,128)}), f32[512,128]{1,0:T(8,128)}) %all-reduce.3.cloned.1.call-update) | async-done | bytes 262160 | tf_op jit(solution)/shard_map/psum | solution.py:11
  849.6 0.0 copy-start.1
  849.6 39.9 %all-gather.11.cloned.1.call-done = f32[1,512,1024]{2,1,0:T(8,128)} async-done(((f32[1,64,1024]{2,1,0:T(8,128)}), f32[1,512,1024]{2,1,0:T(8,128)}) %all-gather.11.cloned.1.call-update) | async-done | bytes 2097168 | tf_op jit(solution)/shard_map/all_gather | solution.py:40
  889.5 0.0 copy-done
  889.5 5.1 fusion.13
  894.6 36.7 %all-gather.13.cloned.1.call-done = f32[1,512,512]{2,1,0:T(8,128)} async-done(((f32[1,64,512]{2,1,0:T(8,128)}), f32[1,512,512]{2,1,0:T(8,128)}) %all-gather.13.cloned.1.call-update) | async-done | bytes 1048592 | tf_op jit(solution)/shard_map/all_gather | solution.py:22
  931.4 2.9 fusion.16
  934.3 0.0 all-reduce.5.cloned.1.call-update
  934.3 0.0 copy-done.1
  934.4 40.0 %all-gather.15.cloned.1.call-done = f32[1,512,1024]{2,1,0:T(8,128)} async-done(((f32[1,64,1024]{2,1,0:T(8,128)}), f32[1,512,1024]{2,1,0:T(8,128)}) %all-gather.15.cloned.1.call-update) | async-done | bytes 2097168 | tf_op jit(solution)/shard_map/all_gather | solution.py:34
  974.4 796.1 %all-reduce.5.cloned.1.call-done = f32[512,128]{1,0:T(8,128)} async-done(((f32[512,128]{1,0:T(8,128)}), f32[512,128]{1,0:T(8,128)}) %all-reduce.5.cloned.1.call-update) | async-done | bytes 262160 | tf_op jit(solution)/shard_map/psum | solution.py:11
  1770.5 0.0 copy-start.2
  1770.5 5.1 fusion.10
  1775.7 0.0 copy-done.2
  1775.7 0.1 slice_select_fusion.1
  1775.7 0.0 copy-start.4
  1775.8 0.8 copy-done.4
  (2 shorter events, 0.0 us)
Async XLA Ops:
  6.5 883.0 %copy-start = (f32[1024,128]{1,0:T(8,128)S(1)}, f32[1024,128]{1,0:T(8,128)}, u32[]{:S(2)}) copy-start(f32[1024,128]{1,0:T(8,128)} %param.3) | copy-start | bytes 1572868
  6.5 50.8 %copy-start.3 = (f32[2,64,1024]{2,1,0:T(8,128)S(1)}, f32[2,64,1024]{2,1,0:T(8,128)}, u32[]{:S(2)}) copy-start(f32[2,64,1024]{2,1,0:T(8,128)} %param.4) | copy-start | bytes 1572868
  6.5 47.7 %all-gather.9.cloned.1.call-start = ((), (), s32[]{:S(2)}) async-start(), calls=%async_computation.2 | async-start | bytes 1179648 | tf_op jit(solution)/shard_map/all_gather | solution.py:22
  8.3 841.3 %all-reduce.3.cloned.1.call-start = ((), (), s32[]{:S(2)}) async-start(), calls=%async_computation | async-start | bytes 524288 | tf_op jit(solution)/shard_map/psum | solution.py:11
  57.3 832.2 %all-gather.11.cloned.1.call-start = ((), (), s32[]{:S(2)}) async-start(), calls=%async_computation.3 | async-start | bytes 2359296 | tf_op jit(solution)/shard_map/all_gather | solution.py:40
  58.2 873.2 %all-gather.13.cloned.1.call-start = ((), (), s32[]{:S(2)}) async-start(), calls=%async_computation.4 | async-start | bytes 1179648 | tf_op jit(solution)/shard_map/all_gather | solution.py:22
  58.7 915.7 %all-gather.15.cloned.1.call-start = ((), (), s32[]{:S(2)}) async-start(), calls=%async_computation.5 | async-start | bytes 2359296 | tf_op jit(solution)/shard_map/all_gather | solution.py:34
  59.3 1711.2 %all-reduce.5.cloned.1.call-start = ((), (), s32[]{:S(2)}) async-start(), calls=%async_computation.1 | async-start | bytes 524288 | tf_op jit(solution)/shard_map/psum | solution.py:11
  849.6 84.7 %copy-start.1 = (f32[512,128]{1,0:T(8,128)S(1)}, f32[512,128]{1,0:T(8,128)}, u32[]{:S(2)}) copy-start(f32[512,128]{1,0:T(8,128)} %all-reduce.3.cloned.1.call-done) | copy-start | bytes 786436
  1770.5 5.2 copy-start.2
  1775.7 0.8 copy-start.4
Sparse Core Ops, SparseCore 0:
  9.4 44.7 all-gather.8
  57.4 792.2 all-reduce.2
  851.9 37.5 all-gather.10
  891.6 39.6 all-gather.12
  933.5 40.8 all-gather.14
  977.4 793.0 all-reduce.4
where the time goes:
time: 1780 us
  waiting for transfers between devices  1750 us (98%)
    psum x2, waiting for transfers between devices, spread(): return lax.psum(jnp.where(mine, array, jnp.zeros_like(array)), axis)  1590 us
    all_gather x2, waiting for transfers between devices, diagonal_solve(): lax.all_gather(inverse_rows, 'cols', axis=0, tiled=True)  82.6 us
    all_gather x1, waiting for transfers between devices, second_update(): lax.all_gather(factor_rows, 'cols', axis=0, tiled=True)  40 us
    all_gather x1, waiting for transfers between devices, on_device(): first_factor = lax.all_gather(factor_panels[0], 'cols', axis=0, tiled=True)  39.9 us
  transfers between devices with their start and end apart: 6, of which 6 were waited for; matrix products, arithmetic and copies ran while one was open for 0% of the time, Pallas kernels for 0%

commit v1 on v0

--- a/solution.py
+++ b/solution.py
@@ -8,7 +8,7 @@
 
 def spread(array, axis, root):
     mine = lax.axis_index(axis) == root
-    return lax.psum(jnp.where(mine, array, jnp.zeros_like(array)), axis)
+    return jnp.sum(lax.all_gather(jnp.where(mine, array, jnp.zeros_like(array)), axis), axis=0)
 
 
 def contract_rows(left, right):

time: 1780 us -> 802 us (0.45)
  the two profiles are of different devices: /device:TPU:16 before, /device:TPU:2 now
where the time goes in v1:
time: 802 us; the launch traced here: 801 us
  waiting for transfers between devices  735 us (92%)
  local copies, waits for them, and re-layouts  21.2 us (3%)
  matrix products  16.2 us (2%)
  other arithmetic  15.5 us (2%)
  between operations  13.5 us (2%)
    all_gather x2, waiting for transfers between devices, spread(): lax.all_gather(jnp.where(mine, array, jnp.zeros_like(array)), axis)  608 us
    all_gather x2, waiting for transfers between devices, diagonal_solve(): lax.all_gather(inverse_rows, 'cols', axis=0, tiled=True)  82.7 us
    all_gather x1, waiting for transfers between devices, on_device(): first_factor = lax.all_gather(factor_panels[0], 'cols', axis=0, tiled=True)  31.9 us
    unnamed x7, local copies, waits for them, and re-layouts  18.5 us
  transfers between devices with their start and end apart: 6, of which 6 were waited for; matrix products, arithmetic and copies ran while one was open for 5% of the time, Pallas kernels for 0%

profile of v1, /device:TPU:2, one launch (start us, length us, event | category | flops | bytes accessed | tf_op | source)
XLA Modules:
  0.0 801.5 jit_solution(3467006127714351804)
XLA Ops:
  6.5 0.0 copy-start.1
  6.5 0.0 all-gather.13.cloned.1.call-start
  6.5 1.7 fusion.22
  8.3 0.0 all-gather.13.cloned.1.call-update
  8.3 0.0 all-gather.15.cloned.1.call-start
  8.4 46.1 %all-gather.13.cloned.1.call-done = f32[1,512,512]{2,1,0:T(8,128)} async-done(((f32[1,64,512]{2,1,0:T(8,128)}), f32[1,512,512]{2,1,0:T(8,128)}) %all-gather.13.cloned.1.call-update) | async-done | bytes 1048592 | tf_op jit(solution)/shard_map/all_gather | solution.py:22
  54.4 3.0 convolution_select_fusion.1
  57.4 0.0 all-gather.15.cloned.1.call-update
  57.4 0.0 all-gather.17.cloned.1.call-start
  57.5 0.0 copy-done.1
  57.5 0.9 fusion.21
  58.3 0.0 all-gather.17.cloned.1.call-update
  58.4 0.0 all-gather.19.cloned.1.call-start
  58.4 0.5 all-gather.19.cloned.1.call-update
  58.9 0.0 all-gather.21.cloned.1.call-start
  59.0 298.0 %all-gather.15.cloned.1.call-done = f32[32768,128]{1,0:T(8,128)} async-done(((f32[512,128]{1,0:T(8,128)}), f32[32768,128]{1,0:T(8,128)}) %all-gather.15.cloned.1.call-update) | async-done | bytes 16777232 | tf_op jit(solution)/shard_map/all_gather | solution.py:11
  357.0 0.0 copy-start
  357.0 6.6 reduce_sum.18
  363.6 31.9 %all-gather.17.cloned.1.call-done = f32[1,512,1024]{2,1,0:T(8,128)} async-done(((f32[1,64,1024]{2,1,0:T(8,128)}), f32[1,512,1024]{2,1,0:T(8,128)}) %all-gather.17.cloned.1.call-update) | async-done | bytes 2097168 | tf_op jit(solution)/shard_map/all_gather | solution.py:40
  395.4 0.0 copy-done
  395.4 5.0 fusion.13
  400.5 36.6 %all-gather.19.cloned.1.call-done = f32[1,512,512]{2,1,0:T(8,128)} async-done(((f32[1,64,512]{2,1,0:T(8,128)}), f32[1,512,512]{2,1,0:T(8,128)}) %all-gather.19.cloned.1.call-update) | async-done | bytes 1048592 | tf_op jit(solution)/shard_map/all_gather | solution.py:22
  437.1 3.2 fusion.16
  440.3 0.0 all-gather.21.cloned.1.call-update
  440.3 0.2 all-gather.23.cloned.1.call-start
  440.5 0.3 all-gather.23.cloned.1.call-update
  440.9 309.7 %all-gather.21.cloned.1.call-done = f32[32768,128]{0,1:T(8,128)} async-done(((f32[512,128]{0,1:T(8,128)}), f32[32768,128]{0,1:T(8,128)}) %all-gather.21.cloned.1.call-update) | async-done | bytes 16777232 | tf_op jit(solution)/shard_map/all_gather | solution.py:11
  750.6 17.7 %copy.11 = f32[16,8,64,512]{3,2,1,0:T(8,128)} copy(f32[16,8,64,512]{3,1,2,0:T(8,128)} %bitcast.39) | data formatting | bytes 33554432
  768.3 8.8 %bitcast_reduce_fusion = f32[512,128]{0,1:T(8,128)S(1)} fusion(f32[16,8,64,512]{3,2,1,0:T(8,128)} %copy.11), kind=kLoop, calls=%fused_computation | loop fusion | flops 4128768 | bytes 17039360 | tf_op jit(solution)/shard_map/reduce_sum | solution.py:11
  777.1 0.1 copy.8
  777.2 11.5 %all-gather.23.cloned.1.call-done = f32[1,512,1024]{2,1,0:T(8,128)} async-done(((f32[1,64,1024]{2,1,0:T(8,128)}), f32[1,512,1024]{2,1,0:T(8,128)}) %all-gather.23.cloned.1.call-update) | async-done | bytes 2097168 | tf_op jit(solution)/shard_map/all_gather | solution.py:34
  788.7 5.0 fusion.10
  793.7 0.1 slice_select_fusion.1
  793.8 0.0 copy-start.2
  793.8 0.8 copy-done.2
  (2 shorter events, 0.0 us)
Async XLA Ops:
  6.5 50.9 %copy-start.1 = (f32[2,64,1024]{2,1,0:T(8,128)S(1)}, f32[2,64,1024]{2,1,0:T(8,128)}, u32[]{:S(2)}) copy-start(f32[2,64,1024]{2,1,0:T(8,128)} %param.4) | copy-start | bytes 1572868
  6.5 47.9 %all-gather.13.cloned.1.call-start = ((), (), s32[]{:S(2)}) async-start(), calls=%async_computation | async-start | bytes 1179648 | tf_op jit(solution)/shard_map/all_gather | solution.py:22
  8.3 348.7 %all-gather.15.cloned.1.call-start = ((), (), s32[]{:S(2)}) async-start(), calls=%async_computation.1 | async-start | bytes 17039360 | tf_op jit(solution)/shard_map/all_gather | solution.py:11
  57.4 338.0 %all-gather.17.cloned.1.call-start = ((), (), s32[]{:S(2)}) async-start(), calls=%async_computation.2 | async-start | bytes 2359296 | tf_op jit(solution)/shard_map/all_gather | solution.py:40
  58.4 378.7 %all-gather.19.cloned.1.call-start = ((), (), s32[]{:S(2)}) async-start(), calls=%async_computation.3 | async-start | bytes 1179648 | tf_op jit(solution)/shard_map/all_gather | solution.py:22
  58.9 691.7 %all-gather.21.cloned.1.call-start = ((), (), s32[]{:S(2)}) async-start(), calls=%async_computation.4 | async-start | bytes 17039360 | tf_op jit(solution)/shard_map/all_gather | solution.py:11
  357.0 38.5 %copy-start = (f32[1024,128]{1,0:T(8,128)S(1)}, f32[1024,128]{1,0:T(8,128)}, u32[]{:S(2)}) copy-start(f32[1024,128]{1,0:T(8,128)} %param.3) | copy-start | bytes 1572868
  440.3 348.4 %all-gather.23.cloned.1.call-start = ((), (), s32[]{:S(2)}) async-start(), calls=%async_computation.5 | async-start | bytes 2359296 | tf_op jit(solution)/shard_map/all_gather | solution.py:34
  793.8 0.8 copy-start.2
Sparse Core Ops, SparseCore 0:
  9.4 44.9 all-gather.12
  59.0 297.9 all-gather.14
  359.1 36.3 all-gather.16
  397.4 39.6 all-gather.18
  441.3 309.2 all-gather.20
  752.5 36.1 all-gather.22
